TPU v7x, 32 devices: a whole 2x2x4 slice. The times are simulated.
32 devices in a mesh: row: 4 (over x, core), grp: 8 (over z, y).
Axes of the slice: x: 2, y: 2, z: 4, core: 2. Of those that a mesh axis runs over, the one named last changes fastest.
Arguments:
- integrals: bfloat16 [32, 512, 256], P('grp', 'row'), may hold values from -1.1953125 to 1.1953125
- amplitudes: bfloat16 [32, 1024, 256], P('grp', 'row'), may hold values from -1.796875 to 1.796875
- pair_orbs: int32 [32, 8], P('grp', 'row'), may hold values from 0 to 3, as said below
- pair_count: int32 [8, 4], P('grp', 'row'), may hold values from 1 to 4, as said below
- neighbours: int32 [32, 16], P('grp', 'row'), may hold values from 0 to 11
- coupling: float32 [32, 16], P('grp', 'row'), may hold values from -1.8 to 1.8
- bases: bfloat16 [32, 1024, 256], P('grp', 'row'), may hold values from -0.375 to 0.375
- virt_energy: float32 [32, 1024], P('grp', 'row'), may hold values from 0.3 to 3
- occ_energy: float32 [32, 4], P('grp', 'row'), may hold values from -1.5 to -0.3
Outputs:
- residual: float32 [32, 1024, 256], P('grp', 'row')
Inputs may be any that keep to these rules, and one draw needn't show every extreme that they name: `pair_orbs`: in the columns of row r the first orbital of every pair is orbital r of the group, the one owned by that device; the second is any orbital of the group. `pair_count`: live slots come first on each device; some device holds 4 live pairs in every draw.
All inputs are finite; a program needn't handle non-finite values.
Results may differ from a plain program's by a relative error of at most 0.0007.
Values may be sent and summed in bfloat16 or wider, within the bound.
No kernel may reach another device: no remote copies, remote signals or barrier semaphores. Data moves between devices by JAX's collectives and lax.ppermute only.
A program may use at most 64 MiB of HBM per device.

v0:
```python
import jax
import jax.numpy as jnp
from jax import lax
from jax.sharding import PartitionSpec as P


def with_halo(array, sides, width):
    for axis, dim in sides:
        count, length = (lax.axis_size(axis), array.shape[dim])
        up = [(i, (i + 1) % count) for i in range(count - 1)]
        down = [(j, i) for i, j in up]
        last = lax.slice_in_dim(array, length - width, length, axis=dim)
        initial = lax.slice_in_dim(array, 0, width, axis=dim)
        before = lax.ppermute(last, axis, up)
        after = lax.ppermute(initial, axis, down)
        array = jnp.concatenate([before, array, after], axis=dim)
    return array


def local(
    integrals,
    amplitudes,
    pair_orbs,
    pair_count,
    neighbours,
    coupling,
    bases,
    virt_energy,
    occ_energy,
):
    width = amplitudes.shape[0]
    live = jnp.arange(width, dtype=jnp.int32) < pair_count[0, 0]
    amps = jnp.where(live[:, None, None], amplitudes, jnp.zeros((), jnp.bfloat16))
    first_orb = pair_orbs[:, 0]
    second_orb = pair_orbs[:, 1]
    piece = lax.all_gather(integrals, "row", axis=1, tiled=True)
    left = jnp.take(piece, first_orb, axis=0)
    right = jnp.take(piece, second_orb, axis=0)
    integ = jnp.einsum("pxa,pxb->pab", left, right, preferred_element_type=jnp.float32)
    first = jnp.einsum("pac,pcd->pad", bases, amps, preferred_element_type=jnp.float32).astype(
        jnp.bfloat16
    )
    moved = jnp.einsum("pad,pbd->pab", first, bases, preferred_element_type=jnp.float32).astype(
        jnp.bfloat16
    )
    window = with_halo(moved, (("grp", 0),), width)
    onehot = (neighbours[:, :, None] == jnp.arange(3 * width, dtype=jnp.int32)).astype(jnp.float32)
    weights = jnp.sum(coupling[:, :, None] * onehot, axis=1)
    combined = jnp.einsum(
        "pm,mab->pab", weights, window.astype(jnp.float32), precision=lax.Precision.HIGHEST
    ).astype(jnp.bfloat16)
    back_first = jnp.einsum(
        "pca,pcb->pab", bases, combined, preferred_element_type=jnp.float32
    ).astype(jnp.bfloat16)
    back = jnp.einsum("pac,pcb->pab", back_first, bases, preferred_element_type=jnp.float32)
    denom = virt_energy[:, :, None] + virt_energy[:, None, :] - occ_energy[:, :, None]
    resid = integ + denom * amps.astype(jnp.float32) - back
    return jnp.where(live[:, None, None], resid, jnp.zeros((), jnp.float32))


def solution(mesh):
    placed = (
        P("grp", "row", None),
        P("grp", "row", None),
        P("grp", "row"),
        P("grp", "row"),
        P("grp", "row"),
        P("grp", "row"),
        P("grp", "row", None),
        P("grp", "row"),
        P("grp", "row"),
    )
    return jax.shard_map(
        local, mesh=mesh, in_specs=placed, out_specs=P("grp", "row", None), check_vma=False
    )
```

profile of v0, /device:TPU:0, one launch (start us, length us, event | category | flops | bytes accessed | tf_op | source)
XLA Modules:
  0.0 52.5 jit_solution(9155367035651967845)
XLA Ops:
  6.5 0.0 copy-start
  6.5 0.0 copy-start.4
  6.5 0.0 copy-start.3
  6.5 0.0 copy-start.2
  6.5 0.0 all-gather.2.cloned.1.call-start
  6.6 0.7 %all-gather.2.cloned.1.call-update = ((bf16[4,128,256]{2,1,0:T(8,128)(2,1)}), bf16[4,512,256]{2,1,0:T(8,128)(2,1)}) async-update(((), (), s32[]{:S(2)}) %all-gather.2.cloned.1.call-start, bf16[4,128,256]{2,1,0:T(8,128)(2,1)} %param.11) | async-update | bytes 1572888
  7.9 0.0 copy-done
  7.9 1.5 %convolution_convert_fusion.2 = bf16[4,256,256]{2,1,0:T(8,128)(2,1)S(1)} fusion(bf16[4,256,256]{2,1,0:T(8,128)(2,1)S(1)} %copy-done, bf16[4,256,256]{2,1,0:T(8,128)(2,1)} %param.12, pred[4]{0:T(512)(128)(4,1)S(1)} %iota_compare_fusion.1), kind=kOutput, calls=%fused_computation.10 | convolution fusion | flops 269221888 | bytes 1572868 | tf_op jit(solution)/shard_map/pad,pbd->pab/dot_general | solution.py:43
  9.5 4.9 %collective-permute-start = (bf16[4,256,256]{2,1,0:T(8,128)(2,1)S(1)}, bf16[4,256,256]{2,1,0:T(8,128)(2,1)S(1)}, u32[]{:S(2)}, u32[]{:S(2)}) collective-permute-start(bf16[4,256,256]{2,1,0:T(8,128)(2,1)S(1)} %convolution_convert_fusion.2), channel_id=1, source_target_pairs={{0,1},{1,2},{2,3},{3,4},{4,5},{5,6},{6,7},{8,9},{9,10},{10,11},{11... | collective-permute-start | bytes 1572872 | tf_op jit(solution)/shard_map/ppermute | solution.py:14
  14.4 1.3 %collective-permute-start.1 = (bf16[4,256,256]{2,1,0:T(8,128)(2,1)S(1)}, bf16[4,256,256]{2,1,0:T(8,128)(2,1)S(1)}, u32[]{:S(2)}, u32[]{:S(2)}) collective-permute-start(bf16[4,256,256]{2,1,0:T(8,128)(2,1)S(1)} %convolution_convert_fusion.2), channel_id=1, source_target_pairs={{1,0},{2,1},{3,2},{4,3},{5,4},{6,5},{7,6},{9,8},{10,9},{11,10},{12... | collective-permute-start | bytes 1572872 | tf_op jit(solution)/shard_map/ppermute | solution.py:15
  15.7 0.0 copy-done.4
  15.8 0.0 copy-done.3
  15.8 0.0 copy-done.2
  15.8 0.1 select_reduce_fusion
  15.9 20.9 %collective-permute-done = bf16[4,256,256]{2,1,0:T(8,128)(2,1)S(1)} collective-permute-done((bf16[4,256,256]{2,1,0:T(8,128)(2,1)S(1)}, bf16[4,256,256]{2,1,0:T(8,128)(2,1)S(1)}, u32[]{:S(2)}, u32[]{:S(2)}) %collective-permute-start) | collective-permute-done | bytes 524320 | tf_op jit(solution)/shard_map/ppermute | solution.py:14
  36.8 0.0 collective-permute-done.1
  36.8 0.2 pad_maximum_fusion
  37.0 1.6 %fusion = bf16[4,256,256]{2,0,1:T(4,128)(2,1)S(1)} fusion(bf16[12,256,256]{2,1,0:T(8,128)(2,1)S(1)} %pad_maximum_fusion, f32[4,12]{1,0:T(4,128)S(1)} %select_reduce_fusion), kind=kOutput, calls=%fused_computation.2 | convolution fusion | flops 37748736 | bytes 2097344 | tf_op jit(solution)/shard_map/pm,mab->pab/dot_general | solution.py:49
  38.6 0.0 all-gather.2.cloned.1.call-done
  38.6 0.0 copy-start.1
  38.6 1.9 %gather_fusion = bf16[4,512,256]{2,1,0:T(8,128)(2,1)S(1)} fusion(bf16[4,512,256]{2,1,0:T(8,128)(2,1)} %all-gather.2.cloned.1.call-done, s32[1024]{0:T(1024)S(1)} %get-tuple-element.13), kind=kCustom, calls=%fused_computation.clone | custom fusion | bytes 2097168 | tf_op jit(solution)/shard_map/jit(_take)/gather | solution.py:37
  40.5 0.0 copy-start.5
  40.6 0.0 copy-start.6
  40.6 0.0 copy-done.1
  40.6 1.6 %gather_fusion.1 = bf16[4,512,256]{2,1,0:T(8,128)(2,1)} fusion(bf16[4,512,256]{2,1,0:T(8,128)(2,1)S(1)} %copy-done.1, s32[1024]{0:T(1024)S(1)} %get-tuple-element.12), kind=kCustom, calls=%fused_computation.1.clone | custom fusion | bytes 2097168 | tf_op jit(solution)/shard_map/jit(_take)/gather | solution.py:38
  42.2 0.0 copy-done.5
  42.2 0.0 copy-done.6
  42.2 2.1 %convolution_add_fusion = f32[4,256,256]{2,1,0:T(8,128)S(1)} fusion(bf16[4,512,256]{2,1,0:T(8,128)(2,1)} %gather_fusion.1, bf16[4,512,256]{2,1,0:T(8,128)(2,1)S(1)} %gather_fusion, pred[4]{0:T(512)(128)(4,1)S(1)} %get-tuple-element.10, pred[4]{0:T(512)(128)(4,1)S(1)} %get-tuple-element.6, f32[4]{0:T(128)S(1)} %bitcast.16, f32[4,256]{1,0:T(4,128)S(1)} %copy-done.5, ...), kind=kOutput, calls=%fused_computation.6 | convolution fusion | flops 271056896 | bytes 3674140 | tf_op jit(solution)/shard_map/pxa,pxb->pab/dot_general | solution.py:39
  44.2 1.5 %fusion.2 = f32[4,256,256]{2,1,0:T(8,128)} fusion(f32[4,256,256]{2,1,0:T(8,128)S(1)} %convolution_add_fusion, bf16[4,256,256]{2,1,0:T(8,128)(2,1)S(1)} %copy-done, bf16[4,256,256]{2,0,1:T(4,128)(2,1)S(1)} %fusion, pred[4]{0:T(512)(128)(4,1)S(1)} %iota_compare_fusion.1), kind=kOutput, calls=%fused_computation.7 | convolution fusion | flops 269221888 | bytes 3145732 | tf_op jit(solution)/shard_map/pac,pcb->pab/dot_general | solution.py:55
  (3 shorter events, 0.0 us)
Async XLA Ops:
  6.5 1.4 %copy-start = (bf16[4,256,256]{2,1,0:T(8,128)(2,1)S(1)}, bf16[4,256,256]{2,1,0:T(8,128)(2,1)}, u32[]{:S(2)}) copy-start(bf16[4,256,256]{2,1,0:T(8,128)(2,1)} %param.17) | copy-start | bytes 1572868
  6.5 9.2 %copy-start.4 = (s32[4,2]{0,1:T(2,128)S(1)}, s32[4,2]{0,1:T(2,128)}, u32[]{:S(2)}) copy-start(s32[4,2]{0,1:T(2,128)} %param.13) | copy-start | bytes 100
  6.5 9.2 %copy-start.3 = (s32[4,4]{1,0:T(4,128)S(1)}, s32[4,4]{1,0:T(4,128)}, u32[]{:S(2)}) copy-start(s32[4,4]{1,0:T(4,128)} %param.15) | copy-start | bytes 196
  6.5 9.3 %copy-start.2 = (f32[4,4]{1,0:T(4,128)S(1)}, f32[4,4]{1,0:T(4,128)}, u32[]{:S(2)}) copy-start(f32[4,4]{1,0:T(4,128)} %param.16) | copy-start | bytes 196
  6.5 32.0 %all-gather.2.cloned.1.call-start = ((), (), s32[]{:S(2)}) async-start(), calls=%async_computation | async-start | bytes 1310720 | tf_op jit(solution)/shard_map/all_gather | solution.py:36
  9.5 27.3 %collective-permute-start = (bf16[4,256,256]{2,1,0:T(8,128)(2,1)S(1)}, bf16[4,256,256]{2,1,0:T(8,128)(2,1)S(1)}, u32[]{:S(2)}, u32[]{:S(2)}) collective-permute-start(bf16[4,256,256]{2,1,0:T(8,128)(2,1)S(1)} %convolution_convert_fusion.2), channel_id=1, source_target_pairs={{0,1},{1,2},{2,3},{3,4},{4,5},{5,6},{6,7},{8,9},{9,10},{10,11},{11... | collective-permute-start | bytes 1572872 | tf_op jit(solution)/shard_map/ppermute | solution.py:14
  14.4 22.4 %collective-permute-start.1 = (bf16[4,256,256]{2,1,0:T(8,128)(2,1)S(1)}, bf16[4,256,256]{2,1,0:T(8,128)(2,1)S(1)}, u32[]{:S(2)}, u32[]{:S(2)}) collective-permute-start(bf16[4,256,256]{2,1,0:T(8,128)(2,1)S(1)} %convolution_convert_fusion.2), channel_id=1, source_target_pairs={{1,0},{2,1},{3,2},{4,3},{5,4},{6,5},{7,6},{9,8},{10,9},{11,10},{12... | collective-permute-start | bytes 1572872 | tf_op jit(solution)/shard_map/ppermute | solution.py:15
  38.6 2.0 %copy-start.1 = (bf16[4,512,256]{2,1,0:T(8,128)(2,1)S(1)}, bf16[4,512,256]{2,1,0:T(8,128)(2,1)}, u32[]{:S(2)}) copy-start(bf16[4,512,256]{2,1,0:T(8,128)(2,1)} %all-gather.2.cloned.1.call-done) | copy-start | bytes 3145732
  40.5 1.6 %copy-start.5 = (f32[4,256]{1,0:T(4,128)S(1)}, f32[4,256]{1,0:T(4,128)}, u32[]{:S(2)}) copy-start(f32[4,256]{1,0:T(4,128)} %param.18) | copy-start | bytes 12292
  40.6 1.6 %copy-start.6 = (f32[4,1]{0,1:T(1,128)S(1)}, f32[4,1]{0,1:T(1,128)}, u32[]{:S(2)}) copy-start(f32[4,1]{0,1:T(1,128)} %param.19) | copy-start | bytes 52
Sparse Core Ops, SparseCore 0:
  8.9 19.4 all-gather.1
where the time goes:
time: 53.4 us; the launch traced here: 52.5 us
  waiting for transfers between devices  21.6 us (40%)
  between operations  14.2 us (27%)
  matrix products  6.64 us (12%)
  starting transfers between devices  6.26 us (12%)
  local copies, waits for them, and re-layouts  3.54 us (7%)
    ppermute x1, waiting for transfers between devices, with_halo(): before = lax.ppermute(last, axis, up)  20.9 us
    ppermute x1, starting transfers between devices, with_halo(): before = lax.ppermute(last, axis, up)  4.94 us
    dot_general x1, matrix products, local(): jnp.einsum('pxa,pxb->pab', left, right, preferred_element_type=jnp.float32)  2.05 us
    gather x1, local copies, waits for them, and re-layouts, local(): left = jnp.take(piece, first_orb, axis=0)  1.93 us
    gather x1, local copies, waits for them, and re-layouts, local(): right = jnp.take(piece, second_orb, axis=0)  1.58 us
    dot_general x1, matrix products, local(): jnp.einsum('pm,mab->pab', weights, window.astype(jnp.float32), precision=...  1.58 us
    dot_general x1, matrix products, local(): jnp.einsum('pad,pbd->pab', first, bases, preferred_element_type=jnp.float32)  1.55 us
    dot_general x1, matrix products, local(): jnp.einsum('pac,pcb->pab', back_first, bases, preferred_element_type=jnp....  1.46 us
  transfers between devices with their start and end apart: 3, of which 1 were waited for; matrix products, arithmetic and copies ran while one was open for 6% of the time, Pallas kernels for 0%

commit v1 on v0

--- a/solution.py
+++ b/solution.py
@@ -3,18 +3,32 @@
 from jax import lax
 from jax.sharding import PartitionSpec as P
 
+CHUNKS = 2
 
-def with_halo(array, sides, width):
-    for axis, dim in sides:
-        count, length = (lax.axis_size(axis), array.shape[dim])
-        up = [(i, (i + 1) % count) for i in range(count - 1)]
+
+def row_gather(array, dim):
+    count = lax.axis_size("row")
+    if count & (count - 1):
+        return lax.all_gather(array, "row", axis=dim, tiled=True)
+    step = count // 2
+    while step:
+        pairs = [(i, i ^ step) for i in range(count)]
+        array = jnp.concatenate([array, lax.ppermute(array, "row", pairs)], axis=dim)
+        step //= 2
+    return array
+
+
+def exchange(moved):
+    count = lax.axis_size("grp")
+    if count % 2:
+        up = [(i, i + 1) for i in range(count - 1)]
         down = [(j, i) for i, j in up]
-        last = lax.slice_in_dim(array, length - width, length, axis=dim)
-        initial = lax.slice_in_dim(array, 0, width, axis=dim)
-        before = lax.ppermute(last, axis, up)
-        after = lax.ppermute(initial, axis, down)
-        array = jnp.concatenate([before, array, after], axis=dim)
-    return array
+        return lax.ppermute(moved, "grp", down), lax.ppermute(moved, "grp", up)
+    swap = [(i, i ^ 1) for i in range(count)]
+    ahead = [(i, i + 2) for i in range(0, count - 2, 2)] + [(i, i - 2) for i in range(3, count, 2)]
+    near = lax.ppermute(moved, "grp", swap)
+    far = lax.ppermute(near, "grp", ahead)
+    return near, far
 
 
 def local(
@@ -33,7 +47,7 @@
     amps = jnp.where(live[:, None, None], amplitudes, jnp.zeros((), jnp.bfloat16))
     first_orb = pair_orbs[:, 0]
     second_orb = pair_orbs[:, 1]
-    piece = lax.all_gather(integrals, "row", axis=1, tiled=True)
+    piece = row_gather(integrals, 1)
     left = jnp.take(piece, first_orb, axis=0)
     right = jnp.take(piece, second_orb, axis=0)
     integ = jnp.einsum("pxa,pxb->pab", left, right, preferred_element_type=jnp.float32)
@@ -43,8 +57,19 @@
     moved = jnp.einsum("pad,pbd->pab", first, bases, preferred_element_type=jnp.float32).astype(
         jnp.bfloat16
     )
-    window = with_halo(moved, (("grp", 0),), width)
-    onehot = (neighbours[:, :, None] == jnp.arange(3 * width, dtype=jnp.int32)).astype(jnp.float32)
+    size = width // CHUNKS if width % CHUNKS == 0 else width
+    near, far = [], []
+    for start in range(0, width, size):
+        got, passed = exchange(moved[start : start + size])
+        near.append(got)
+        far.append(passed)
+    window = jnp.concatenate(near + [moved] + far, axis=0)
+    even = lax.axis_index("grp") % 2 == 0
+    if lax.axis_size("grp") % 2:
+        even = jnp.bool_(True)
+    block = neighbours // width
+    place = jnp.where(even, 2 - block, block) * width + neighbours % width
+    onehot = (place[:, :, None] == jnp.arange(3 * width, dtype=jnp.int32)).astype(jnp.float32)
     weights = jnp.sum(coupling[:, :, None] * onehot, axis=1)
     combined = jnp.einsum(
         "pm,mab->pab", weights, window.astype(jnp.float32), precision=lax.Precision.HIGHEST

time: 53.4 us -> 39.7 us (0.74); the launches traced: 52.5 us -> 39.5 us
  between operations: 14.2 us -> 0.88 us
  waiting for transfers between devices: 21.6 us -> 13 us
  starting transfers between devices: 6.26 us -> 12.2 us
  matrix products: 6.64 us -> 7.89 us
  local copies, waits for them, and re-layouts: 3.54 us -> 4.55 us
  other arithmetic: 0.29 us -> 0.95 us
    ppermute x2 -> x6, waiting for transfers between devices: 20.9 us -> 13 us  [the longest x2 7.43 us: exchange(): far = lax.ppermute(near, 'grp', ahead)]
    ppermute x2 -> x6, starting transfers between devices: 6.23 us -> 12.2 us  [the longest x2 7.18 us: exchange(): far = lax.ppermute(near, 'grp', ahead)]
    unnamed x14 -> x22, local copies, waits for them, and re-layouts: 0.03 us -> 1.45 us
    gather x1, local copies, waits for them, and re-layouts: 1.93 us -> 0.61 us  [local(): left = jnp.take(piece, first_orb, axis=0)]
    dot_general x1, matrix products: 2.05 us -> 3.25 us  [local(): jnp.einsum('pxa,pxb->pab', left, right, preferred_element_type=jnp.float32)]
    slice x0 -> x1, local copies, waits for them, and re-layouts: none -> 0.84 us  [local(): got, passed = exchange(moved[start:start + size])]
    unnamed x1 -> x0, waiting for transfers between devices: 0.68 us -> none
    concatenate x1, other arithmetic: 0.17 us -> 0.83 us  [row_gather(): jnp.concatenate([array, lax.ppermute(array, 'row', pairs)], axis=dim)]
  transfers between devices with their start and end apart: 3 -> 6, of which waited for: 1 -> 3; matrix products, arithmetic and copies ran while one was open for 6% -> 13% of each run, Pallas kernels for 0% -> 0%
where the time goes in v1:
time: 39.7 us; the launch traced here: 39.5 us
  waiting for transfers between devices  13 us (33%)
  starting transfers between devices  12.2 us (31%)
  matrix products  7.89 us (20%)
  local copies, waits for them, and re-layouts  4.55 us (11%)
  other arithmetic  0.95 us (2%)
  between operations  0.88 us (2%)
    ppermute x2, waiting for transfers between devices, exchange(): far = lax.ppermute(near, 'grp', ahead)  7.43 us
    ppermute x2, starting transfers between devices, exchange(): far = lax.ppermute(near, 'grp', ahead)  7.18 us
    ppermute x2, waiting for transfers between devices, row_gather(): lax.ppermute(array, 'row', pairs)  5.61 us
    dot_general x1, matrix products, local(): jnp.einsum('pxa,pxb->pab', left, right, preferred_element_type=jnp.float32)  3.25 us
    ppermute x2, starting transfers between devices, exchange(): near = lax.ppermute(moved, 'grp', swap)  3.03 us
    ppermute x2, starting transfers between devices, row_gather(): lax.ppermute(array, 'row', pairs)  1.98 us
    gather x1, local copies, waits for them, and re-layouts, local(): right = jnp.take(piece, second_orb, axis=0)  1.6 us
    dot_general x1, matrix products, local(): jnp.einsum('pad,pbd->pab', first, bases, preferred_element_type=jnp.float32)  1.59 us
  transfers between devices with their start and end apart: 6, of which 3 were waited for; matrix products, arithmetic and copies ran while one was open for 13% of the time, Pallas kernels for 0%

profile of v1, /device:TPU:0, one launch (start us, length us, event | category | flops | bytes accessed | tf_op | source)
XLA Modules:
  0.0 39.5 jit_solution(16688464534516913506)
XLA Ops:
  0.0 0.0 copy-start
  0.7 0.3 copy-done
  1.1 0.0 copy-start.1
  1.1 0.0 copy-start.4
  1.1 0.0 copy-start.3
  1.1 0.0 copy-start.2
  1.1 1.6 %convolution_convert_fusion.2 = bf16[4,256,256]{2,1,0:T(8,128)(2,1)S(1)} fusion(bf16[4,256,256]{2,1,0:T(8,128)(2,1)S(1)} %copy-done, bf16[4,256,256]{2,1,0:T(8,128)(2,1)} %param.12, pred[4]{0:T(512)(128)(4,1)S(1)} %iota_compare_fusion.1), kind=kOutput, calls=%fused_computation.9 | convolution fusion | flops 269221888 | bytes 1572868 | tf_op jit(solution)/shard_map/pad,pbd->pab/dot_general | solution.py:57
  2.7 0.8 %fusion.18 = (bf16[2,256,256]{2,1,0:T(8,128)(2,1)}, bf16[2,256,256]{2,1,0:T(8,128)(2,1)}) fusion(bf16[4,256,256]{2,1,0:T(8,128)(2,1)S(1)} %convolution_convert_fusion.2), kind=kLoop, calls=%fused_computation.50 | loop fusion | bytes 1048576 | tf_op jit(solution)/shard_map/slice | solution.py:63
  3.5 3.0 %collective-permute-start.2 = (bf16[2,256,256]{2,1,0:T(8,128)(2,1)}, bf16[2,256,256]{2,1,0:T(8,128)(2,1)}, u32[]{:S(2)}, u32[]{:S(2)}) collective-permute-start(bf16[2,256,256]{2,1,0:T(8,128)(2,1)} %get-tuple-element.11), channel_id=1, source_target_pairs={{0,1},{1,0},{2,3},{3,2},{4,5},{5,4},{6,7},{7,6},{8,9},{9,8},{10,11... | collective-permute-start | bytes 786440 | tf_op jit(solution)/shard_map/ppermute | solution.py:29
  6.5 0.0 collective-permute-start.3
  6.5 0.0 copy-done.1
  6.5 2.0 %collective-permute-start = (bf16[4,128,256]{2,1,0:T(8,128)(2,1)S(1)}, bf16[4,128,256]{2,1,0:T(8,128)(2,1)S(1)}, u32[]{:S(2)}, u32[]{:S(2)}) collective-permute-start(bf16[4,128,256]{2,1,0:T(8,128)(2,1)S(1)} %copy-done.1), channel_id=1, source_target_pairs={{0,16},{8,24},{16,0},{24,8},{1,17},{9,25},{17,1},{25,9},{2,18},{10... | collective-permute-start | bytes 786440 | tf_op jit(solution)/shard_map/ppermute | solution.py:16
  8.5 0.0 copy-done.4
  8.5 0.0 copy-done.3
  8.6 0.0 copy-done.2
  8.6 0.1 select_reduce_fusion
  8.7 5.6 %collective-permute-done = bf16[4,128,256]{2,1,0:T(8,128)(2,1)S(1)} collective-permute-done((bf16[4,128,256]{2,1,0:T(8,128)(2,1)S(1)}, bf16[4,128,256]{2,1,0:T(8,128)(2,1)S(1)}, u32[]{:S(2)}, u32[]{:S(2)}) %collective-permute-start) | collective-permute-done | bytes 262176 | tf_op jit(solution)/shard_map/ppermute | solution.py:16
  14.3 0.8 %pad_maximum_fusion = bf16[4,256,256]{2,1,0:T(8,128)(2,1)} fusion(bf16[4,128,256]{2,1,0:T(8,128)(2,1)S(1)} %collective-permute-done, bf16[4,128,256]{2,1,0:T(8,128)(2,1)S(1)} %copy-done.1), kind=kLoop, calls=%fused_computation.16 | loop fusion | flops 1048576 | bytes 1048576 | tf_op jit(solution)/shard_map/concatenate | solution.py:16
  15.1 0.0 collective-permute-start.1
  15.1 0.0 collective-permute-done.2
  15.1 3.7 %collective-permute-start.4 = (bf16[2,256,256]{2,1,0:T(8,128)(2,1)}, bf16[2,256,256]{2,1,0:T(8,128)(2,1)S(1)}, u32[]{:S(2)}, u32[]{:S(2)}) collective-permute-start(bf16[2,256,256]{2,1,0:T(8,128)(2,1)} %collective-permute-done.2), channel_id=1, source_target_pairs={{0,2},{2,4},{4,6},{3,1},{5,3},{7,5},{8,10},{10,12},{12,14},{11,9},... | collective-permute-start | bytes 786440 | tf_op jit(solution)/shard_map/ppermute | solution.py:30
  18.8 1.0 %constant_dynamic-update-slice_fusion.7 = bf16[12,256,256]{2,1,0:T(8,128)(2,1)S(1)} fusion(bf16[2,256,256]{2,1,0:T(8,128)(2,1)} %collective-permute-done.2), kind=kLoop, calls=%fused_computation.26 | loop fusion | bytes 524288
  19.8 0.0 collective-permute-done.3
  19.8 3.5 %collective-permute-start.5 = (bf16[2,256,256]{2,1,0:T(8,128)(2,1)S(1)}, bf16[2,256,256]{2,1,0:T(8,128)(2,1)S(1)}, u32[]{:S(2)}, u32[]{:S(2)}) collective-permute-start(bf16[2,256,256]{2,1,0:T(8,128)(2,1)S(1)} %collective-permute-done.3), channel_id=1, source_target_pairs={{0,2},{2,4},{4,6},{3,1},{5,3},{7,5},{8,10},{10,12},{12,14},{11,9},... | collective-permute-start | bytes 786440 | tf_op jit(solution)/shard_map/ppermute | solution.py:30
  23.4 2.4 %collective-permute-done.4 = bf16[2,256,256]{2,1,0:T(8,128)(2,1)S(1)} collective-permute-done((bf16[2,256,256]{2,1,0:T(8,128)(2,1)}, bf16[2,256,256]{2,1,0:T(8,128)(2,1)S(1)}, u32[]{:S(2)}, u32[]{:S(2)}) %collective-permute-start.4) | collective-permute-done | bytes 262176 | tf_op jit(solution)/shard_map/ppermute | solution.py:30
  25.8 5.0 %collective-permute-done.5 = bf16[2,256,256]{2,1,0:T(8,128)(2,1)S(1)} collective-permute-done((bf16[2,256,256]{2,1,0:T(8,128)(2,1)S(1)}, bf16[2,256,256]{2,1,0:T(8,128)(2,1)S(1)}, u32[]{:S(2)}, u32[]{:S(2)}) %collective-permute-start.5) | collective-permute-done | bytes 262176 | tf_op jit(solution)/shard_map/ppermute | solution.py:30
  30.9 1.6 %fusion = bf16[4,256,256]{2,0,1:T(4,128)(2,1)S(1)} fusion(bf16[12,256,256]{2,1,0:T(8,128)(2,1)S(1)} %constant_dynamic-update-slice_fusion.3, f32[4,12]{1,0:T(4,128)S(1)} %select_reduce_fusion), kind=kOutput, calls=%fused_computation.2 | convolution fusion | flops 37748736 | bytes 2097344 | tf_op jit(solution)/shard_map/pm,mab->pab/dot_general | solution.py:74
  32.5 1.5 %fusion.4 = f32[4,256,256]{2,1,0:T(8,128)} fusion(bf16[4,256,256]{2,1,0:T(8,128)(2,1)S(1)} %copy-done, bf16[4,256,256]{2,0,1:T(4,128)(2,1)S(1)} %fusion), kind=kOutput, calls=%fused_computation.10 | convolution fusion | flops 268697600 | bytes 2097152 | tf_op jit(solution)/shard_map/pac,pcb->pab/dot_general | solution.py:80
  33.9 0.0 collective-permute-done.1
  34.0 0.6 %gather_fusion = bf16[4,512,256]{2,1,0:T(8,128)(2,1)S(1)} fusion(bf16[4,512,256]{2,1,0:T(8,128)(2,1)S(1)} %constant_dynamic-update-slice_fusion, s32[1024]{0:T(1024)S(1)} %get-tuple-element.15), kind=kCustom, calls=%fused_computation.clone | custom fusion | bytes 2097168 | tf_op jit(solution)/shard_map/jit(_take)/gather | solution.py:51
  34.6 0.0 copy-start.5
  34.6 0.0 copy-start.6
  34.6 0.0 copy-start.7
  34.6 1.6 %gather_fusion.1 = bf16[4,512,256]{2,1,0:T(8,128)(2,1)} fusion(bf16[4,512,256]{2,1,0:T(8,128)(2,1)S(1)} %constant_dynamic-update-slice_fusion, s32[1024]{0:T(1024)S(1)} %get-tuple-element.14), kind=kCustom, calls=%fused_computation.1.clone | custom fusion | bytes 2097168 | tf_op jit(solution)/shard_map/jit(_take)/gather | solution.py:52
  36.2 0.0 copy-done.5
  36.2 0.0 copy-done.6
  36.2 0.0 copy-done.7
  36.2 3.3 %fusion.3 = f32[4,256,256]{2,1,0:T(8,128)} fusion(f32[4,256,256]{2,1,0:T(8,128)} %fusion.4, bf16[4,512,256]{2,1,0:T(8,128)(2,1)} %gather_fusion.1, bf16[4,512,256]{2,1,0:T(8,128)(2,1)S(1)} %gather_fusion, pred[4]{0:T(512)(128)(4,1)S(1)} %get-tuple-element.12, pred[4]{0:T(512)(128)(4,1)S(1)} %get-tuple-element.6, f32[4]{0:T(128)S(1)} %bitcast.16, ...), kind=kOutput, calls=%fused_computation.6 | convolution fusion | flops 271581184 | bytes 4722716 | tf_op jit(solution)/shard_map/pxa,pxb->pab/dot_general | solution.py:53
  (11 shorter events, 0.2 us)
Async XLA Ops:
  0.0 1.1 %copy-start = (bf16[4,256,256]{2,1,0:T(8,128)(2,1)S(1)}, bf16[4,256,256]{2,1,0:T(8,128)(2,1)}, u32[]{:S(2)}) copy-start(bf16[4,256,256]{2,1,0:T(8,128)(2,1)} %param.17) | copy-start | bytes 1572868
  1.1 5.5 %copy-start.1 = (bf16[4,128,256]{2,1,0:T(8,128)(2,1)S(1)}, bf16[4,128,256]{2,1,0:T(8,128)(2,1)}, u32[]{:S(2)}) copy-start(bf16[4,128,256]{2,1,0:T(8,128)(2,1)} %param.11) | copy-start | bytes 786436
  1.1 7.4 %copy-start.4 = (s32[4,2]{0,1:T(2,128)S(1)}, s32[4,2]{0,1:T(2,128)}, u32[]{:S(2)}) copy-start(s32[4,2]{0,1:T(2,128)} %param.13) | copy-start | bytes 100
  1.1 7.5 %copy-start.3 = (s32[4,4]{1,0:T(4,128)S(1)}, s32[4,4]{1,0:T(4,128)}, u32[]{:S(2)}) copy-start(s32[4,4]{1,0:T(4,128)} %param.15) | copy-start | bytes 196
  1.1 7.5 %copy-start.2 = (f32[4,4]{1,0:T(4,128)S(1)}, f32[4,4]{1,0:T(4,128)}, u32[]{:S(2)}) copy-start(f32[4,4]{1,0:T(4,128)} %param.16) | copy-start | bytes 196
  3.5 11.6 %collective-permute-start.2 = (bf16[2,256,256]{2,1,0:T(8,128)(2,1)}, bf16[2,256,256]{2,1,0:T(8,128)(2,1)}, u32[]{:S(2)}, u32[]{:S(2)}) collective-permute-start(bf16[2,256,256]{2,1,0:T(8,128)(2,1)} %get-tuple-element.11), channel_id=1, source_target_pairs={{0,1},{1,0},{2,3},{3,2},{4,5},{5,4},{6,7},{7,6},{8,9},{9,8},{10,11... | collective-permute-start | bytes 786440 | tf_op jit(solution)/shard_map/ppermute | solution.py:29
  6.5 13.3 %collective-permute-start.3 = (bf16[2,256,256]{2,1,0:T(8,128)(2,1)}, bf16[2,256,256]{2,1,0:T(8,128)(2,1)S(1)}, u32[]{:S(2)}, u32[]{:S(2)}) collective-permute-start(bf16[2,256,256]{2,1,0:T(8,128)(2,1)} %get-tuple-element.10), channel_id=1, source_target_pairs={{0,1},{1,0},{2,3},{3,2},{4,5},{5,4},{6,7},{7,6},{8,9},{9,8},{10,11... | collective-permute-start | bytes 786440 | tf_op jit(solution)/shard_map/ppermute | solution.py:29
  6.5 7.8 %collective-permute-start = (bf16[4,128,256]{2,1,0:T(8,128)(2,1)S(1)}, bf16[4,128,256]{2,1,0:T(8,128)(2,1)S(1)}, u32[]{:S(2)}, u32[]{:S(2)}) collective-permute-start(bf16[4,128,256]{2,1,0:T(8,128)(2,1)S(1)} %copy-done.1), channel_id=1, source_target_pairs={{0,16},{8,24},{16,0},{24,8},{1,17},{9,25},{17,1},{25,9},{2,18},{10... | collective-permute-start | bytes 786440 | tf_op jit(solution)/shard_map/ppermute | solution.py:16
  15.1 18.8 %collective-permute-start.1 = (bf16[4,256,256]{2,1,0:T(8,128)(2,1)}, bf16[4,256,256]{2,1,0:T(8,128)(2,1)S(1)}, u32[]{:S(2)}, u32[]{:S(2)}) collective-permute-start(bf16[4,256,256]{2,1,0:T(8,128)(2,1)} %pad_maximum_fusion), channel_id=1, source_target_pairs={{0,8},{8,0},{16,24},{24,16},{1,9},{9,1},{17,25},{25,17},{2,10},{10... | collective-permute-start | bytes 1572872 | tf_op jit(solution)/shard_map/ppermute | solution.py:16
  15.1 10.7 %collective-permute-start.4 = (bf16[2,256,256]{2,1,0:T(8,128)(2,1)}, bf16[2,256,256]{2,1,0:T(8,128)(2,1)S(1)}, u32[]{:S(2)}, u32[]{:S(2)}) collective-permute-start(bf16[2,256,256]{2,1,0:T(8,128)(2,1)} %collective-permute-done.2), channel_id=1, source_target_pairs={{0,2},{2,4},{4,6},{3,1},{5,3},{7,5},{8,10},{10,12},{12,14},{11,9},... | collective-permute-start | bytes 786440 | tf_op jit(solution)/shard_map/ppermute | solution.py:30
  19.8 11.0 %collective-permute-start.5 = (bf16[2,256,256]{2,1,0:T(8,128)(2,1)S(1)}, bf16[2,256,256]{2,1,0:T(8,128)(2,1)S(1)}, u32[]{:S(2)}, u32[]{:S(2)}) collective-permute-start(bf16[2,256,256]{2,1,0:T(8,128)(2,1)S(1)} %collective-permute-done.3), channel_id=1, source_target_pairs={{0,2},{2,4},{4,6},{3,1},{5,3},{7,5},{8,10},{10,12},{12,14},{11,9},... | collective-permute-start | bytes 786440 | tf_op jit(solution)/shard_map/ppermute | solution.py:30
  34.6 1.6 %copy-start.5 = (bf16[4,256,256]{2,1,0:T(8,128)(2,1)S(1)}, bf16[4,256,256]{2,1,0:T(8,128)(2,1)}, u32[]{:S(2)}) copy-start(bf16[4,256,256]{2,1,0:T(8,128)(2,1)} %param.12) | copy-start | bytes 1572868
  34.6 1.6 %copy-start.6 = (f32[4,256]{1,0:T(4,128)S(1)}, f32[4,256]{1,0:T(4,128)}, u32[]{:S(2)}) copy-start(f32[4,256]{1,0:T(4,128)} %param.18) | copy-start | bytes 12292
  34.6 1.6 %copy-start.7 = (f32[4,1]{0,1:T(1,128)S(1)}, f32[4,1]{0,1:T(1,128)}, u32[]{:S(2)}) copy-start(f32[4,1]{0,1:T(1,128)} %param.19) | copy-start | bytes 52

commit v2 on v0

v2 whole, which is shorter than its diff:
```python
import functools

import jax
import jax.numpy as jnp
from jax import lax
from jax.experimental import pallas as pl
from jax.experimental.pallas import tpu as pltpu
from jax.sharding import PartitionSpec as P


BF16 = jnp.bfloat16
F32 = jnp.float32
VMEM = pltpu.VMEM
SMEM = pltpu.SMEM
HBM = pltpu.HBM
GRANT = 8 << 20


def dot(a, b, dims):
    return lax.dot_general(a, b, (dims, ((), ())), preferred_element_type=F32)


def call(kernel, outs, inputs, flops, scratch=(), aliases=()):
    values, specs = [], []
    for space, value in inputs:
        if space in (VMEM, HBM):
            value = pltpu.with_memory_space_constraint(value, space)
        values.append(value)
        specs.append(pl.BlockSpec(memory_space=space))
    shapes, out_specs = [], []
    for space, shape, dtype in outs:
        plain = space is pl.ANY
        shapes.append(jax.ShapeDtypeStruct(shape, dtype) if plain else space(shape, dtype))
        out_specs.append(pl.BlockSpec(memory_space=space))
    size = sum(value.size * value.dtype.itemsize for value in values)
    return pl.pallas_call(
        kernel,
        out_shape=shapes,
        in_specs=specs,
        out_specs=out_specs,
        scratch_shapes=scratch,
        input_output_aliases=dict(aliases),
        cost_estimate=pl.CostEstimate(flops=flops, bytes_accessed=16 * size, transcendentals=0),
        compiler_params=pltpu.CompilerParams(vmem_limit_bytes=GRANT),
    )(*values)


def transform(base, amp):
    first = dot(base, amp, ((1,), (0,))).astype(BF16)
    return dot(first, base, ((1,), (1,))).astype(BF16)


def lead_kernel(count, amps, bases, *refs):
    small = (len(refs) - 6) // 2
    sources, (out, amps_out, bases_out, count_out) = refs[:small], refs[small : small + 4]
    targets, (number, sems) = refs[small + 4 : -2], refs[-2:]
    width = amps.shape[0]
    first = pltpu.make_async_copy(count, number, sems.at[2, 0])
    loads = [
        [
            pltpu.make_async_copy(bases.at[slot], bases_out.at[slot], sems.at[0, slot]),
            pltpu.make_async_copy(amps.at[slot], amps_out.at[slot], sems.at[1, slot]),
        ]
        for slot in range(width)
    ]
    others = [
        pltpu.make_async_copy(source, target, sems.at[3, n])
        for n, (source, target) in enumerate(zip(sources, targets))
    ]
    for load in loads[0] + [first] + sum(loads[1:], []) + others:
        load.start()
    for load in loads[0]:
        load.wait()
    out[...] = transform(bases_out[0], amps_out[0])
    first.wait()
    count_out[...] = jnp.full(count_out.shape, number[0, 0], jnp.int32)
    for load in sum(loads[1:], []) + others:
        load.wait()


def rest_kernel(count, amps, bases, *outs):
    for slot, out in enumerate(outs, 1):
        live = jnp.where(slot < count[...], jnp.float32(1), jnp.float32(0)).astype(BF16)
        out[...] = transform(bases[slot], amps[slot] * live)


def integ_kernel(orbs, occ, energy, amps, *refs):
    pieces, (out, held, sems) = refs[:-3], refs[-3:]
    width = amps.shape[0]
    column = energy[...].T
    left = jnp.concatenate([piece[orbs[0, 0]] for piece in pieces], axis=0).T
    stores = []
    for slot in range(width):
        right = jnp.concatenate([piece[orbs[1, slot]] for piece in pieces], axis=0)
        denom = column[:, slot : slot + 1] + energy[slot : slot + 1, :] - occ[0, slot]
        integ = dot(left, right, ((1,), (0,)))
        held[slot] = integ + denom * amps[slot].astype(F32)
        stores.append(pltpu.make_async_copy(held.at[slot], out.at[slot], sems.at[slot]))
        stores[slot].start()
    for store in stores:
        store.wait()


def add_tiles(rows, columns, weights, tiles, out, before=None):
    width, height = out.shape[0], out.shape[1]
    total = weights.shape[0] // width

    def step(block, carry):
        at = pl.ds(pl.multiple_of(block * rows, rows), rows)
        values = [tile[at, :].astype(F32) for tile in tiles]
        for slot in range(width):
            acc = None if before is None else before[slot, at, :]
            for m, value in zip(columns, values):
                row = slot * total + m
                term = weights[row : row + 1, :] * value
                acc = term if acc is None else acc + term
            out[slot, at, :] = acc
        return carry

    lax.fori_loop(0, height // rows, step, 0)


def gather_kernel(columns, weights, *refs):
    add_tiles(16, columns, weights, refs[:-1], refs[-1])


def final_kernel(columns, count, weights, base, bases, sums, *refs):
    tiles, (out, held, sems) = refs[:-3], refs[-3:]
    width = base.shape[0]
    half = width // 2
    total = weights.shape[0] // width
    loads = [pltpu.make_async_copy(base.at[s], held.at[s], sems.at[0, s]) for s in range(width)]
    stores = [pltpu.make_async_copy(held.at[s], out.at[s], sems.at[1, s]) for s in range(width)]
    for load in loads:
        load.start()
    number = jnp.max(count[...])

    def some(slots):
        combined = []
        for slot in slots:
            acc = sums[slot]
            for m, tile in zip(columns, tiles):
                row = slot * total + m
                acc = acc + weights[row : row + 1, :] * tile[...].astype(F32)
            combined.append(acc.astype(BF16))
        firsts = [dot(bases[s], c, ((0,), (0,))).astype(BF16) for s, c in zip(slots, combined)]
        for slot, first in zip(slots, firsts):
            back = dot(first, bases[slot], ((1,), (0,)))
            live = jnp.broadcast_to(slot < count[...], back.shape)
            loads[slot].wait()
            held[slot] = jnp.where(live, held[slot] - back, jnp.float32(0))
            stores[slot].start()

    some(range(half))

    @pl.when(number > half)
    def _():
        some(range(half, width))

    @pl.when(number <= half)
    def _():
        for slot in range(half, width):
            loads[slot].wait()
            held[slot] = jnp.zeros(held.shape[1:], F32)
            stores[slot].start()

    for store in stores:
        store.wait()


def row_pieces(array):
    count = lax.axis_size("row")
    pieces = [array]
    if count & (count - 1):
        for shift in range(1, count):
            pairs = [(i, (i + shift) % count) for i in range(count)]
            pieces.append(lax.ppermute(array, "row", pairs))
        return pieces
    step = count // 2
    while step:
        pairs = [(i, i ^ step) for i in range(count)]
        pieces += [lax.ppermute(piece, "row", pairs) for piece in pieces]
        step //= 2
    return pieces


def tile_weights(neighbours, coupling, width, virt):
    levels = lax.axis_size("grp") // 2
    group = lax.axis_index("grp")
    level = lax.shift_right_logical(group, 1)
    even = (group & 1) == 0
    odd_level = (level & 1) == 1
    inside = jnp.where(even, level > 0, level < levels - 1)
    tail = jnp.where(odd_level == even, 3 * width - 1, 3 * width)
    block = (neighbours >= width).astype(jnp.int32) + (neighbours >= 2 * width).astype(jnp.int32)
    kind = jnp.where(even, 2 - block, block)
    scale = jnp.where((kind < 2) | inside, coupling, 0.0)
    place = neighbours + (kind - block) * width
    place = jnp.where(place == 3 * width - 1, tail, place)
    total = 3 * width + 1
    shape = (width, total, virt, neighbours.shape[1])
    index = lax.broadcasted_iota(jnp.int32, shape, 1)
    hit = place[:, None, None, :] == index
    table = jnp.sum(jnp.where(hit, scale[:, None, None, :], 0.0), axis=3)
    return table.reshape(width * total, virt)


def level_pairs(count, phase):
    half = count // 2
    other = []
    for z in range(half):
        mate = z ^ 1 if phase == 0 else (z + 1 if z % 2 else z - 1)
        other.append(mate if 0 <= mate < half else z)
    return [(2 * z + y, 2 * other[z] + y) for z in range(half) for y in range(2)]


def local(
    integrals,
    amplitudes,
    pair_orbs,
    pair_count,
    neighbours,
    coupling,
    bases,
    virt_energy,
    occ_energy,
):
    width, virt = amplitudes.shape[0], amplitudes.shape[1]
    count = lax.axis_size("grp")
    cube = 2 * virt * virt * virt
    tile = (VMEM, (virt, virt), BF16)
    stack = (VMEM, (width, virt, virt), BF16)
    wide = (VMEM, (width, virt, virt), F32)
    last = width - 1
    dma = pltpu.SemaphoreType.DMA

    small = (neighbours, coupling, virt_energy, pair_orbs.T, occ_energy.T)
    own, amps, basis, counts, *small = call(
        lead_kernel,
        [tile, stack, stack, (VMEM, (1, virt), jnp.int32)]
        + [(VMEM, value.shape, value.dtype) for value in small],
        [(pl.ANY, pair_count), (HBM, amplitudes), (HBM, bases)] + [(HBM, value) for value in small],
        2 * cube, [SMEM((1, 1), jnp.int32), dma((4, max(width, len(small))))],
    )
    neighbours, coupling, virt_energy, orbs, occ = small
    own = [own] + list(call(
        rest_kernel, [tile] * last, [(VMEM, counts), (VMEM, amps), (VMEM, basis)],
        2 * last * cube,
    ))
    weights = tile_weights(neighbours, coupling, width, virt)

    swap = [(i, i ^ 1) for i in range(count)]
    ring = [(i, (i + 2) % count if i % 2 == 0 else (i - 2) % count) for i in range(count)]
    near = [lax.ppermute(t, "grp", swap) for t in own]
    far = [lax.ppermute(near[n], "grp", ring) for n in range(last)]
    far_a = lax.ppermute(near[last], "grp", level_pairs(count, 0))
    far_b = lax.ppermute(near[last], "grp", level_pairs(count, 1))

    pieces = row_pieces(integrals)
    aux = sum(piece.shape[1] for piece in pieces)
    base = call(
        integ_kernel, [(HBM, (width, virt, virt), F32)],
        [(SMEM, orbs), (SMEM, occ), (VMEM, virt_energy), (VMEM, amplitudes)]
        + [(VMEM, piece) for piece in pieces], 2 * width * virt * virt * aux,
        [VMEM((width, virt, virt), F32), dma((width,))],
    )[0]
    sums = call(
        functools.partial(gather_kernel, range(3 * width - 1)), [wide],
        [(VMEM, weights)] + [(VMEM, t) for t in near + own + far], 8 * width * virt * virt,
    )[0]
    return call(
        functools.partial(final_kernel, (3 * width - 1, 3 * width)),
        [(pl.ANY, (width, virt, virt), F32)],
        [(VMEM, counts), (VMEM, weights), (HBM, base), (VMEM, bases), (VMEM, sums),
         (VMEM, far_a), (VMEM, far_b)],
        2 * width * cube, [VMEM((width, virt, virt), F32), dma((2, width))],
    )[0]


def solution(mesh):
    placed = (
        P("grp", "row", None),
        P("grp", "row", None),
        P("grp", "row"),
        P("grp", "row"),
        P("grp", "row"),
        P("grp", "row"),
        P("grp", "row", None),
        P("grp", "row"),
        P("grp", "row"),
    )

    return jax.shard_map(
        local, mesh=mesh, in_specs=placed, out_specs=P("grp", "row", None), check_vma=False
    )
```

time: 53.4 us -> 32.4 us (0.61); the launches traced: 52.5 us -> 32.2 us
  between operations: 14.2 us -> 0.78 us
  waiting for transfers between devices: 21.6 us -> 11.4 us
  Pallas kernels: 0 us -> 7.12 us
  matrix products: 6.64 us -> 0 us
  starting transfers between devices: 6.26 us -> 12.7 us
  local copies, waits for them, and re-layouts: 3.54 us -> 0.03 us
    ppermute x2 -> x12, waiting for transfers between devices: 20.9 us -> 11.4 us  [the longest x4 6.34 us: local(): near = [lax.ppermute(t, 'grp', swap) for t in own]]
    pallas_call x0 -> x5, Pallas kernels: none -> 7.12 us  [call(): pl.pallas_call(kernel, out_shape=shapes, in_specs=specs, out_specs=out_sp...]
    dot_general x4 -> x0, matrix products: 6.64 us -> none  [the longest x1 2.05 us: local(): jnp.einsum('pxa,pxb->pab', left, right, preferred_element_type=jnp.float32)]
    ppermute x2 -> x12, starting transfers between devices: 6.23 us -> 12.7 us  [the longest x3 4.73 us: local(): far = [lax.ppermute(near[n], 'grp', ring) for n in range(last)]]
    gather x2 -> x0, local copies, waits for them, and re-layouts: 3.51 us -> none  [the longest x1 1.93 us: local(): left = jnp.take(piece, first_orb, axis=0)]
    unnamed x1 -> x0, waiting for transfers between devices: 0.68 us -> none
  transfers between devices with their start and end apart: 3 -> 12, of which waited for: 1 -> 6; matrix products, arithmetic and copies ran while one was open for 6% -> 1% of each run, Pallas kernels for 0% -> 15%
where the time goes in v2:
time: 32.4 us; the launch traced here: 32.2 us
  starting transfers between devices  12.7 us (39%)
  waiting for transfers between devices  11.4 us (35%)
  Pallas kernels  7.12 us (22%)
  between operations  0.78 us (2%)
    pallas_call x5, Pallas kernels, call(): pl.pallas_call(kernel, out_shape=shapes, in_specs=specs, out_specs=out_sp...  7.12 us
    ppermute x4, waiting for transfers between devices, local(): near = [lax.ppermute(t, 'grp', swap) for t in own]  6.34 us
    ppermute x3, waiting for transfers between devices, local(): far = [lax.ppermute(near[n], 'grp', ring) for n in range(last)]  5.04 us
    ppermute x3, starting transfers between devices, local(): far = [lax.ppermute(near[n], 'grp', ring) for n in range(last)]  4.73 us
    ppermute x4, starting transfers between devices, local(): near = [lax.ppermute(t, 'grp', swap) for t in own]  4.12 us
    ppermute x3, starting transfers between devices, row_pieces(): pieces += [lax.ppermute(piece, 'row', pairs) for piece in pieces]  2.97 us
    ppermute x1, starting transfers between devices, local(): far_b = lax.ppermute(near[last], 'grp', level_pairs(count, 1))  0.66 us
  transfers between devices with their start and end apart: 12, of which 6 were waited for; matrix products, arithmetic and copies ran while one was open for 1% of the time, Pallas kernels for 15%

profile of v2, /device:TPU:0, one launch (start us, length us, event | category | flops | bytes accessed | tf_op | source)
XLA Modules:
  0.0 32.2 jit_solution(2334052211758846913)
XLA Ops:
  0.0 3.0 %collective-permute-start = (bf16[4,128,256]{2,1,0:T(8,128)(2,1)}, bf16[4,128,256]{2,1,0:T(8,128)(2,1)S(1)}, u32[]{:S(2)}, u32[]{:S(2)}) collective-permute-start(bf16[4,128,256]{2,1,0:T(8,128)(2,1)} %refs_0_.3), channel_id=1, source_target_pairs={{0,16},{8,24},{16,0},{24,8},{1,17},{9,25},{17,1},{25,9},{2,18},{10... | collective-permute-start | bytes 786440 | tf_op jit(solution)/shard_map/ppermute | solution.py:182
  3.6 1.5 %shard_map.91 = (bf16[256,256]{1,0:T(8,128)(2,1)S(1)}, bf16[4,256,256]{2,1,0:T(8,128)(2,1)S(1)}, bf16[4,256,256]{2,1,0:T(8,128)(2,1)S(1)}, s32[1,256]{1,0:T(1,12...) custom-call(s32[1,1]{1,0:T(1,128)S(6)} %copy.10.count, ...), custom_call_target="tpu_custom_call" | custom-call | flops 67108864 | bytes 16845632 | tf_op jit(solution)/shard_map/pallas_call | solution.py:36
  5.1 0.0 copy-start.2
  5.2 0.5 %shard_map.93 = (bf16[256,256]{1,0:T(8,128)(2,1)S(1)}, bf16[256,256]{1,0:T(8,128)(2,1)S(1)}, bf16[256,256]{1,0:T(8,128)(2,1)S(1)}) custom-call(s32[1,256]{1,0:T(1,128)S(1)} %get-tuple-element.17.count, bf16[4,256,256]{2,1,0:T(8,128)(2,1)S(1)} %get-tuple-element.24.amps, bf16[4,256,256]{2,1,0:T(8,128)(2,1)S(1)} %get-tuple-element.25.bases), custom_call_target="tpu_custom_call" | custom-call | flops 201326592 | bytes 16793600 | tf_op jit(solution)/shard_map/pallas_call | solution.py:36
  5.6 1.6 %collective-permute-start.6 = (bf16[256,256]{1,0:T(8,128)(2,1)S(1)}, bf16[256,256]{1,0:T(8,128)(2,1)S(1)}, u32[]{:S(2)}, u32[]{:S(2)}) collective-permute-start(bf16[256,256]{1,0:T(8,128)(2,1)S(1)} %get-tuple-element.28.refs_7_), channel_id=1, source_target_pairs={{0,1},{1,0},{2,3},{3,2},{4,5},{5,4},{6,7},{7,6},{8,9},{9,8},{10,11... | collective-permute-start | bytes 393224 | tf_op jit(solution)/shard_map/ppermute | solution.py:254
  7.2 0.5 %collective-permute-start.4 = (bf16[256,256]{1,0:T(8,128)(2,1)S(1)}, bf16[256,256]{1,0:T(8,128)(2,1)S(1)}, u32[]{:S(2)}, u32[]{:S(2)}) collective-permute-start(bf16[256,256]{1,0:T(8,128)(2,1)S(1)} %get-tuple-element.26.refs_5_), channel_id=1, source_target_pairs={{0,1},{1,0},{2,3},{3,2},{4,5},{5,4},{6,7},{7,6},{8,9},{9,8},{10,11... | collective-permute-start | bytes 393224 | tf_op jit(solution)/shard_map/ppermute | solution.py:254
  7.7 1.5 %collective-permute-start.5 = (bf16[256,256]{1,0:T(8,128)(2,1)S(1)}, bf16[256,256]{1,0:T(8,128)(2,1)S(1)}, u32[]{:S(2)}, u32[]{:S(2)}) collective-permute-start(bf16[256,256]{1,0:T(8,128)(2,1)S(1)} %get-tuple-element.27.refs_6_), channel_id=1, source_target_pairs={{0,1},{1,0},{2,3},{3,2},{4,5},{5,4},{6,7},{7,6},{8,9},{9,8},{10,11... | collective-permute-start | bytes 393224 | tf_op jit(solution)/shard_map/ppermute | solution.py:254
  9.3 0.5 %collective-permute-start.3 = (bf16[256,256]{1,0:T(8,128)(2,1)S(1)}, bf16[256,256]{1,0:T(8,128)(2,1)S(1)}, u32[]{:S(2)}, u32[]{:S(2)}) collective-permute-start(bf16[256,256]{1,0:T(8,128)(2,1)S(1)} %get-tuple-element.23.refs_4_), channel_id=1, source_target_pairs={{0,1},{1,0},{2,3},{3,2},{4,5},{5,4},{6,7},{7,6},{8,9},{9,8},{10,11... | collective-permute-start | bytes 393224 | tf_op jit(solution)/shard_map/ppermute | solution.py:254
  9.8 2.3 %collective-permute-done.6.refs_3_ = bf16[256,256]{1,0:T(8,128)(2,1)S(1)} collective-permute-done((bf16[256,256]{1,0:T(8,128)(2,1)S(1)}, bf16[256,256]{1,0:T(8,128)(2,1)S(1)}, u32[]{:S(2)}, u32[]{:S(2)}) %collective-permute-start.6) | collective-permute-done | bytes 131104 | tf_op jit(solution)/shard_map/ppermute | solution.py:254
  12.1 0.0 copy-done.2
  12.1 0.0 collective-permute-start.1
  12.1 2.8 %collective-permute-done.4.refs_1_ = bf16[256,256]{1,0:T(8,128)(2,1)S(1)} collective-permute-done((bf16[256,256]{1,0:T(8,128)(2,1)S(1)}, bf16[256,256]{1,0:T(8,128)(2,1)S(1)}, u32[]{:S(2)}, u32[]{:S(2)}) %collective-permute-start.4) | collective-permute-done | bytes 131104 | tf_op jit(solution)/shard_map/ppermute | solution.py:254
  14.9 1.6 %collective-permute-start.8 = (bf16[256,256]{1,0:T(8,128)(2,1)S(1)}, bf16[256,256]{1,0:T(8,128)(2,1)S(1)}, u32[]{:S(2)}, u32[]{:S(2)}) collective-permute-start(bf16[256,256]{1,0:T(8,128)(2,1)S(1)} %collective-permute-done.4.refs_1_), channel_id=1, source_target_pairs={{0,2},{1,7},{2,4},{3,1},{4,6},{5,3},{6,0},{7,5},{8,10},{9,15},{10,... | collective-permute-start | bytes 393224 | tf_op jit(solution)/shard_map/ppermute | solution.py:255
  16.5 1.2 %collective-permute-done.5.refs_2_ = bf16[256,256]{1,0:T(8,128)(2,1)S(1)} collective-permute-done((bf16[256,256]{1,0:T(8,128)(2,1)S(1)}, bf16[256,256]{1,0:T(8,128)(2,1)S(1)}, u32[]{:S(2)}, u32[]{:S(2)}) %collective-permute-start.5) | collective-permute-done | bytes 131104 | tf_op jit(solution)/shard_map/ppermute | solution.py:254
  17.7 1.6 %collective-permute-start.9 = (bf16[256,256]{1,0:T(8,128)(2,1)S(1)}, bf16[256,256]{1,0:T(8,128)(2,1)S(1)}, u32[]{:S(2)}, u32[]{:S(2)}) collective-permute-start(bf16[256,256]{1,0:T(8,128)(2,1)S(1)} %collective-permute-done.5.refs_2_), channel_id=1, source_target_pairs={{0,2},{1,7},{2,4},{3,1},{4,6},{5,3},{6,0},{7,5},{8,10},{9,15},{10,... | collective-permute-start | bytes 393224 | tf_op jit(solution)/shard_map/ppermute | solution.py:255
  19.3 0.0 collective-permute-done.3.refs_0_
  19.3 1.6 %collective-permute-start.7 = (bf16[256,256]{1,0:T(8,128)(2,1)S(1)}, bf16[256,256]{1,0:T(8,128)(2,1)S(1)}, u32[]{:S(2)}, u32[]{:S(2)}) collective-permute-start(bf16[256,256]{1,0:T(8,128)(2,1)S(1)} %collective-permute-done.3.refs_0_), channel_id=1, source_target_pairs={{0,2},{1,7},{2,4},{3,1},{4,6},{5,3},{6,0},{7,5},{8,10},{9,15},{10,... | collective-permute-start | bytes 393224 | tf_op jit(solution)/shard_map/ppermute | solution.py:255
  20.9 0.0 collective-permute-done.refs_1_
  20.9 0.0 collective-permute-start.2
  20.9 1.4 %collective-permute-done.8.refs_9_ = bf16[256,256]{1,0:T(8,128)(2,1)S(1)} collective-permute-done((bf16[256,256]{1,0:T(8,128)(2,1)S(1)}, bf16[256,256]{1,0:T(8,128)(2,1)S(1)}, u32[]{:S(2)}, u32[]{:S(2)}) %collective-permute-start.8) | collective-permute-done | bytes 131104 | tf_op jit(solution)/shard_map/ppermute | solution.py:255
  22.3 0.3 collective-permute-start.10
  22.5 2.6 %collective-permute-done.9.refs_10_ = bf16[256,256]{1,0:T(8,128)(2,1)S(1)} collective-permute-done((bf16[256,256]{1,0:T(8,128)(2,1)S(1)}, bf16[256,256]{1,0:T(8,128)(2,1)S(1)}, u32[]{:S(2)}, u32[]{:S(2)}) %collective-permute-start.9) | collective-permute-done | bytes 131104 | tf_op jit(solution)/shard_map/ppermute | solution.py:255
  25.2 0.7 %collective-permute-start.11 = (bf16[256,256]{1,0:T(8,128)(2,1)S(1)}, bf16[256,256]{1,0:T(8,128)(2,1)S(1)}, u32[]{:S(2)}, u32[]{:S(2)}) collective-permute-start(bf16[256,256]{1,0:T(8,128)(2,1)S(1)} %collective-permute-done.6.refs_3_), channel_id=1, source_target_pairs={{0,0},{1,1},{2,4},{3,5},{4,2},{5,3},{6,6},{7,7},{8,8},{9,9},{10,12... | collective-permute-start | bytes 393224 | tf_op jit(solution)/shard_map/ppermute | solution.py:257
  25.8 0.2 select_reduce_fusion
  26.0 0.0 copy-start.1
  26.0 1.0 %collective-permute-done.7.refs_8_ = bf16[256,256]{1,0:T(8,128)(2,1)S(1)} collective-permute-done((bf16[256,256]{1,0:T(8,128)(2,1)S(1)}, bf16[256,256]{1,0:T(8,128)(2,1)S(1)}, u32[]{:S(2)}, u32[]{:S(2)}) %collective-permute-start.7) | collective-permute-done | bytes 131104 | tf_op jit(solution)/shard_map/ppermute | solution.py:255
  27.0 1.0 %shard_map.94.sums = f32[4,256,256]{2,1,0:T(8,128)S(1)} custom-call(f32[52,256]{1,0:T(8,128)S(1)} %reshape.5.weights, bf16[256,256]{1,0:T(8,128)(2,1)S(1)} %collective-permute-done.3.refs_0_, bf16[256,256]{1,0:T(8,128)(2,1)S(1)} %collective-permute-done.4.refs_1_, bf16[256,256]{1,0:T(8,128)(2,1)S(1)} %collective-permute-done.5.refs_2_, ...), custom_call_target="tpu_custom_call" | custom-call | flops 2097152 | bytes 23920640 | tf_op jit(solution)/shard_map/pallas_call | solution.py:36
  28.0 0.0 collective-permute-done.1.refs_2_
  28.0 0.0 collective-permute-done.2.refs_3_
  28.0 0.0 copy-done.1
  28.1 0.0 copy-start
  28.1 2.0 %shard_map.92.base = f32[4,256,256]{2,1,0:T(8,128)} custom-call(s32[2,4]{1,0:T(2,128)S(1)} %get-tuple-element.20.orbs, f32[1,4]{1,0:T(1,128)S(1)} %get-tuple-element.21.occ, f32[4,256]{1,0:T(4,128)S(1)} %get-tuple-element.22.energy, bf16[4,256,256]{2,1,0:T(8,128)(2,1)S(1)} %copy-done.1, bf16[4,128,256]{2,1,0:T(8,128)(2,1)S(1)} %copy-done.2, ...), custom_call_target="tpu_custom_call" | custom-call | flops 268435456 | bytes 25232128 | tf_op jit(solution)/shard_map/pallas_call | solution.py:36
  30.1 0.0 collective-permute-done.10.refs_0_
  30.1 0.0 collective-permute-done.11.refs_1_
  30.1 0.0 copy-done
  30.1 2.1 %shard_map.95 = f32[4,256,256]{2,1,0:T(8,128)} custom-call(s32[1,256]{1,0:T(1,128)S(1)} %get-tuple-element.17.count, f32[52,256]{1,0:T(8,128)S(1)} %reshape.5.weights, f32[4,256,256]{2,1,0:T(8,128)} %shard_map.92.base, bf16[4,256,256]{2,1,0:T(8,128)(2,1)S(1)} %copy-done, f32[4,256,256]{2,1,0:T(8,128)S(1)} %shard_map.94.sums, ...), custom_call_target="tpu_custom_call" | custom-call | flops 268435456 | bytes 47005696 | tf_op jit(solution)/shard_map/pallas_call | solution.py:36
  (3 shorter events, 0.0 us)
Async XLA Ops:
  0.0 20.9 %collective-permute-start = (bf16[4,128,256]{2,1,0:T(8,128)(2,1)}, bf16[4,128,256]{2,1,0:T(8,128)(2,1)S(1)}, u32[]{:S(2)}, u32[]{:S(2)}) collective-permute-start(bf16[4,128,256]{2,1,0:T(8,128)(2,1)} %refs_0_.3), channel_id=1, source_target_pairs={{0,16},{8,24},{16,0},{24,8},{1,17},{9,25},{17,1},{25,9},{2,18},{10... | collective-permute-start | bytes 786440 | tf_op jit(solution)/shard_map/ppermute | solution.py:182
  5.1 6.9 %copy-start.2 = (bf16[4,128,256]{2,1,0:T(8,128)(2,1)S(1)}, bf16[4,128,256]{2,1,0:T(8,128)(2,1)}, u32[]{:S(2)}) copy-start(bf16[4,128,256]{2,1,0:T(8,128)(2,1)} %refs_0_.3) | copy-start | bytes 786436
  5.6 6.4 %collective-permute-start.6 = (bf16[256,256]{1,0:T(8,128)(2,1)S(1)}, bf16[256,256]{1,0:T(8,128)(2,1)S(1)}, u32[]{:S(2)}, u32[]{:S(2)}) collective-permute-start(bf16[256,256]{1,0:T(8,128)(2,1)S(1)} %get-tuple-element.28.refs_7_), channel_id=1, source_target_pairs={{0,1},{1,0},{2,3},{3,2},{4,5},{5,4},{6,7},{7,6},{8,9},{9,8},{10,11... | collective-permute-start | bytes 393224 | tf_op jit(solution)/shard_map/ppermute | solution.py:254
  7.2 7.7 %collective-permute-start.4 = (bf16[256,256]{1,0:T(8,128)(2,1)S(1)}, bf16[256,256]{1,0:T(8,128)(2,1)S(1)}, u32[]{:S(2)}, u32[]{:S(2)}) collective-permute-start(bf16[256,256]{1,0:T(8,128)(2,1)S(1)} %get-tuple-element.26.refs_5_), channel_id=1, source_target_pairs={{0,1},{1,0},{2,3},{3,2},{4,5},{5,4},{6,7},{7,6},{8,9},{9,8},{10,11... | collective-permute-start | bytes 393224 | tf_op jit(solution)/shard_map/ppermute | solution.py:254
  7.7 10.0 %collective-permute-start.5 = (bf16[256,256]{1,0:T(8,128)(2,1)S(1)}, bf16[256,256]{1,0:T(8,128)(2,1)S(1)}, u32[]{:S(2)}, u32[]{:S(2)}) collective-permute-start(bf16[256,256]{1,0:T(8,128)(2,1)S(1)} %get-tuple-element.27.refs_6_), channel_id=1, source_target_pairs={{0,1},{1,0},{2,3},{3,2},{4,5},{5,4},{6,7},{7,6},{8,9},{9,8},{10,11... | collective-permute-start | bytes 393224 | tf_op jit(solution)/shard_map/ppermute | solution.py:254
  9.3 10.0 %collective-permute-start.3 = (bf16[256,256]{1,0:T(8,128)(2,1)S(1)}, bf16[256,256]{1,0:T(8,128)(2,1)S(1)}, u32[]{:S(2)}, u32[]{:S(2)}) collective-permute-start(bf16[256,256]{1,0:T(8,128)(2,1)S(1)} %get-tuple-element.23.refs_4_), channel_id=1, source_target_pairs={{0,1},{1,0},{2,3},{3,2},{4,5},{5,4},{6,7},{7,6},{8,9},{9,8},{10,11... | collective-permute-start | bytes 393224 | tf_op jit(solution)/shard_map/ppermute | solution.py:254
  12.1 15.9 %collective-permute-start.1 = (bf16[4,128,256]{2,1,0:T(8,128)(2,1)S(1)}, bf16[4,128,256]{2,1,0:T(8,128)(2,1)S(1)}, u32[]{:S(2)}, u32[]{:S(2)}) collective-permute-start(bf16[4,128,256]{2,1,0:T(8,128)(2,1)S(1)} %copy-done.2), channel_id=1, source_target_pairs={{0,8},{8,0},{16,24},{24,16},{1,9},{9,1},{17,25},{25,17},{2,10},{10... | collective-permute-start | bytes 786440 | tf_op jit(solution)/shard_map/ppermute | solution.py:182
  14.9 7.4 %collective-permute-start.8 = (bf16[256,256]{1,0:T(8,128)(2,1)S(1)}, bf16[256,256]{1,0:T(8,128)(2,1)S(1)}, u32[]{:S(2)}, u32[]{:S(2)}) collective-permute-start(bf16[256,256]{1,0:T(8,128)(2,1)S(1)} %collective-permute-done.4.refs_1_), channel_id=1, source_target_pairs={{0,2},{1,7},{2,4},{3,1},{4,6},{5,3},{6,0},{7,5},{8,10},{9,15},{10,... | collective-permute-start | bytes 393224 | tf_op jit(solution)/shard_map/ppermute | solution.py:255
  17.7 7.5 %collective-permute-start.9 = (bf16[256,256]{1,0:T(8,128)(2,1)S(1)}, bf16[256,256]{1,0:T(8,128)(2,1)S(1)}, u32[]{:S(2)}, u32[]{:S(2)}) collective-permute-start(bf16[256,256]{1,0:T(8,128)(2,1)S(1)} %collective-permute-done.5.refs_2_), channel_id=1, source_target_pairs={{0,2},{1,7},{2,4},{3,1},{4,6},{5,3},{6,0},{7,5},{8,10},{9,15},{10,... | collective-permute-start | bytes 393224 | tf_op jit(solution)/shard_map/ppermute | solution.py:255
  19.3 7.8 %collective-permute-start.7 = (bf16[256,256]{1,0:T(8,128)(2,1)S(1)}, bf16[256,256]{1,0:T(8,128)(2,1)S(1)}, u32[]{:S(2)}, u32[]{:S(2)}) collective-permute-start(bf16[256,256]{1,0:T(8,128)(2,1)S(1)} %collective-permute-done.3.refs_0_), channel_id=1, source_target_pairs={{0,2},{1,7},{2,4},{3,1},{4,6},{5,3},{6,0},{7,5},{8,10},{9,15},{10,... | collective-permute-start | bytes 393224 | tf_op jit(solution)/shard_map/ppermute | solution.py:255
  20.9 7.2 %collective-permute-start.2 = (bf16[4,128,256]{2,1,0:T(8,128)(2,1)S(1)}, bf16[4,128,256]{2,1,0:T(8,128)(2,1)S(1)}, u32[]{:S(2)}, u32[]{:S(2)}) collective-permute-start(bf16[4,128,256]{2,1,0:T(8,128)(2,1)S(1)} %collective-permute-done.refs_1_), channel_id=1, source_target_pairs={{0,8},{8,0},{16,24},{24,16},{1,9},{9,1},{17,25},{25,17},{2,10},{10... | collective-permute-start | bytes 786440 | tf_op jit(solution)/shard_map/ppermute | solution.py:182
  22.3 7.8 %collective-permute-start.10 = (bf16[256,256]{1,0:T(8,128)(2,1)S(1)}, bf16[256,256]{1,0:T(8,128)(2,1)S(1)}, u32[]{:S(2)}, u32[]{:S(2)}) collective-permute-start(bf16[256,256]{1,0:T(8,128)(2,1)S(1)} %collective-permute-done.6.refs_3_), channel_id=1, source_target_pairs={{0,2},{1,3},{2,0},{3,1},{4,6},{5,7},{6,4},{7,5},{8,10},{9,11},{10,... | collective-permute-start | bytes 393224 | tf_op jit(solution)/shard_map/ppermute | solution.py:256
  25.2 4.9 %collective-permute-start.11 = (bf16[256,256]{1,0:T(8,128)(2,1)S(1)}, bf16[256,256]{1,0:T(8,128)(2,1)S(1)}, u32[]{:S(2)}, u32[]{:S(2)}) collective-permute-start(bf16[256,256]{1,0:T(8,128)(2,1)S(1)} %collective-permute-done.6.refs_3_), channel_id=1, source_target_pairs={{0,0},{1,1},{2,4},{3,5},{4,2},{5,3},{6,6},{7,7},{8,8},{9,9},{10,12... | collective-permute-start | bytes 393224 | tf_op jit(solution)/shard_map/ppermute | solution.py:257
  26.0 2.0 %copy-start.1 = (bf16[4,256,256]{2,1,0:T(8,128)(2,1)S(1)}, bf16[4,256,256]{2,1,0:T(8,128)(2,1)}, u32[]{:S(2)}) copy-start(bf16[4,256,256]{2,1,0:T(8,128)(2,1)} %amps.3) | copy-start | bytes 1572868
  28.1 2.0 %copy-start = (bf16[4,256,256]{2,1,0:T(8,128)(2,1)S(1)}, bf16[4,256,256]{2,1,0:T(8,128)(2,1)}, u32[]{:S(2)}) copy-start(bf16[4,256,256]{2,1,0:T(8,128)(2,1)} %bases.3) | copy-start | bytes 1572868
